TPU v7x, 32 devices: a whole 2x2x4 slice. The times are simulated.
32 devices in a mesh: row: 8 (over y, x, core), col: 4 (over z).
Axes of the slice: x: 2, y: 2, z: 4, core: 2. Of those that a mesh axis runs over, the one named last changes fastest.
Arguments:
- upper_blocks: bfloat16 [64, 8, 128, 128], P('row', None, 'col'), as said below
- block_cols: int32 [64, 8], replicated, may hold values from -1 to 63, as said below
- filter_cols: int32 [64, 8], replicated, may hold values from -1 to 63, as said below
Outputs:
- purified: float32 [64, 8, 128, 128], P('row', None, 'col')
Inputs may be any that keep to these rules, and one draw needn't show every extreme that they name: `block_cols`: slot 0 of row i holds i; every other slot holds -1 or a block column j with i < j < i + 8 and j < 64; the columns of a row are distinct; rows i <= 56 have no -1. `filter_cols`: slot 0 of row i holds i; every other slot holds -1 or a block column j with i < j < i + 8 and j < 64; the columns of a row are distinct; rows i <= 56 have no -1. Every diagonal block upper_blocks[i, 0] is symmetric.
All inputs are finite; a program needn't handle non-finite values.
Results may differ from a plain program's by a relative error of at most 0.002.
Values may be sent and summed in bfloat16 or wider, within the bound.
A program may use at most 128 MiB of HBM per device.

v0:
```python
import jax
import jax.numpy as jnp
from jax import lax
from jax.sharding import PartitionSpec as P

B = 128
W = 8
row_group = 4


def padded(value, sides, width):
    for axis, dim in sides:
        devices, length = (lax.axis_size(axis), value.shape[dim])
        up = [(i, (i + 1) % devices) for i in range(devices - 1)]
        down = [(j, i) for i, j in up]
        last = lax.slice_in_dim(value, length - width, length, axis=dim)
        leading = lax.slice_in_dim(value, 0, width, axis=dim)
        before = lax.ppermute(last, axis, up)
        after = lax.ppermute(leading, axis, down)
        value = jnp.concatenate([before, value, after], axis=dim)
    return value


def from_behind(value, axis, steps):
    count = lax.axis_size(axis)
    leading, last = (max(0, -steps), min(count, count - steps))
    return lax.ppermute(value, axis, [(source, source + steps) for source in range(leading, last)])


def band_right(blocks, columns, first_row):
    count_rows = blocks.shape[0]
    rim_rows = W - 1
    count_cols = count_rows - rim_rows
    first_col = first_row + rim_rows
    column_ids = first_col + jnp.arange(count_cols, dtype=jnp.int32)
    row_labels = first_row + jnp.arange(count_rows, dtype=jnp.int32)
    upper_hit = (columns[:, :, None] == column_ids[None, None, :]).astype(jnp.bfloat16)
    upper_part = jnp.einsum(
        "akxy,akb->axby", blocks, upper_hit, preferred_element_type=jnp.bfloat16
    )
    source = columns[rim_rows:]
    lower_hit = (source[:, :, None] == row_labels[None, None, :]) & (
        source[:, :, None] > column_ids[:, None, None]
    )
    lower_part = jnp.einsum(
        "bkxy,bka->aybx",
        blocks[rim_rows:],
        lower_hit.astype(jnp.bfloat16),
        preferred_element_type=jnp.bfloat16,
    )
    return upper_part + lower_part


def left_from_filter(own_slots, own_targets, mirror_slots, mirror_targets, first_row, row_count):
    rim_rows = W - 1
    count_cols = row_count + 2 * rim_rows
    band_ids = first_row + jnp.arange(count_cols, dtype=jnp.int32)
    own_ids = first_row + rim_rows + jnp.arange(row_count, dtype=jnp.int32)
    upper_hit = (own_targets[:, :, None] == band_ids[None, None, :]).astype(jnp.bfloat16)
    upper_part = jnp.einsum(
        "ifxy,ifa->ixay", own_slots, upper_hit, preferred_element_type=jnp.bfloat16
    )
    mirror_ids = first_row + jnp.arange(row_count + rim_rows, dtype=jnp.int32)
    lower_hit = (mirror_targets[:, :, None] == own_ids[None, None, :]) & (
        mirror_targets[:, :, None] > mirror_ids[:, None, None]
    )
    lower_part = jnp.einsum(
        "mfxy,mfi->ixmy",
        mirror_slots,
        lower_hit.astype(jnp.bfloat16),
        preferred_element_type=jnp.bfloat16,
    )
    lower_part = jnp.pad(lower_part, ((0, 0), (0, 0), (0, rim_rows), (0, 0)))
    return upper_part + lower_part


def pick_slots(product, targets, first_col):
    column_ids = first_col + jnp.arange(product.shape[2], dtype=jnp.int32)
    selector = (targets[:, :, None] == column_ids[None, None, :]).astype(jnp.float32)
    return jnp.einsum(
        "ixby,ifb->ifxy",
        product,
        selector,
        precision=lax.Precision.HIGHEST,
        preferred_element_type=jnp.float32,
    )


def group_products(left_rows, right_band, targets, first_col):
    outputs = []
    row_count = left_rows.shape[0]
    inner_rows = left_rows.shape[1]
    span_rows = row_group + 2 * (W - 1)
    width_cols = row_group + W - 1
    for group_index in range(row_count // row_group):
        row_start = group_index * row_group
        left_part = left_rows[
            row_start : row_start + row_group, :, row_start : row_start + span_rows, :
        ]
        left_part = left_part.reshape(row_group * inner_rows, span_rows * B)
        right_part = right_band[
            row_start : row_start + span_rows, :, row_start : row_start + width_cols, :
        ]
        right_part = right_part.reshape(span_rows * B, width_cols * B)
        product = jnp.dot(left_part, right_part, preferred_element_type=jnp.float32)
        product = product.reshape(row_group, inner_rows, width_cols, B)
        outputs.append(
            pick_slots(product, targets[row_start : row_start + row_group], first_col + row_start)
        )
    return jnp.concatenate(outputs, axis=0)


def per_device(upper_blocks, block_cols, filter_cols):
    rim_rows = W - 1
    row_count = upper_blocks.shape[0]
    quarter = upper_blocks.shape[2]
    row_first = lax.axis_index("row") * row_count
    col_first = lax.axis_index("col") * quarter
    padded_cols = jnp.pad(block_cols, ((rim_rows, rim_rows), (0, 0)), constant_values=-1)
    padded_filter = jnp.pad(filter_cols, ((rim_rows, 0), (0, 0)), constant_values=-1)
    window_cols = lax.dynamic_slice_in_dim(padded_cols, row_first, row_count + 2 * rim_rows, 0)
    window_filter = lax.dynamic_slice_in_dim(padded_filter, row_first, row_count + rim_rows, 0)
    own_filter = lax.dynamic_slice_in_dim(filter_cols, row_first, row_count, 0)
    whole_blocks = lax.all_gather(upper_blocks, "col", axis=2, tiled=True)
    window_blocks = padded(whole_blocks, (("row", 0),), rim_rows)
    band_first = row_first - rim_rows
    right_band = band_right(window_blocks, window_cols, band_first)
    own_band = lax.dynamic_slice_in_dim(right_band[:, :, :row_count, :], col_first, quarter, 3)
    left_rows = jnp.transpose(own_band, (2, 3, 0, 1))
    square = group_products(left_rows, right_band, own_filter, row_first)
    square_half = square.astype(jnp.bfloat16)
    whole_square = lax.all_gather(square_half, "col", axis=2, tiled=True)
    earlier = from_behind(whole_square[row_count - rim_rows :], "row", 1)
    joined = jnp.concatenate([earlier, whole_square], axis=0)
    mirror_cols = lax.dynamic_slice_in_dim(joined, col_first, quarter, 3)
    mirror_slots = jnp.swapaxes(mirror_cols, 2, 3)
    left_filter = left_from_filter(
        square_half, own_filter, mirror_slots, window_filter, band_first, row_count
    )
    cube_terms = group_products(left_filter, right_band, own_filter, row_first)
    return 3.0 * square - 2.0 * cube_terms


def solution(mesh):
    return jax.shard_map(
        per_device,
        mesh=mesh,
        in_specs=(P("row", None, "col", None), P(), P()),
        out_specs=P("row", None, "col", None),
        check_vma=False,
    )
```

profile of v0, /device:TPU:4, one launch (start us, length us, event | category | flops | bytes accessed | tf_op | source)
XLA Modules:
  0.0 327.1 jit_solution(9591159979319002050)
XLA Ops:
  8.7 47.4 %all-gather.3.cloned.1.call-done = bf16[8,8,128,128]{3,1,2,0:T(8,128)(2,1)} async-done(((bf16[8,8,32,128]{3,1,2,0:T(8,128)(2,1)}), bf16[8,8,128,128]{3,1,2,0:T(8,128)(2,1)}) %all-gather.3.cloned.1.call-update) | async-done | bytes 2097168 | tf_op jit(solution)/shard_map/all_gather | solution.py:124
  56.1 4.3 %fusion.70 = (bf16[7,8,128,128]{3,1,2,0:T(8,128)(2,1)}, bf16[7,8,128,128]{3,1,2,0:T(8,128)(2,1)}) fusion(bf16[8,8,128,128]{3,1,2,0:T(8,128)(2,1)} %all-gather.3.cloned.1.call-done), kind=kLoop, calls=%fused_computation.90 | loop fusion | bytes 7340032 | tf_op jit(solution)/shard_map/slice | solution.py:16
  66.0 35.9 %collective-permute-done.1 = bf16[7,8,128,128]{3,1,2,0:T(8,128)(2,1)} collective-permute-done((bf16[7,8,128,128]{3,1,2,0:T(8,128)(2,1)}, bf16[7,8,128,128]{3,1,2,0:T(8,128)(2,1)}, u32[]{:S(2)}, u32[]{:S(2)}) %collective-permute-start.1) | collective-permute-done | bytes 1835040 | tf_op jit(solution)/shard_map/ppermute | solution.py:19
  101.9 7.3 %fusion.7 = bf16[15,22,128,128]{3,1,2,0:T(8,128)(2,1)} fusion(bf16[7,8,128,128]{3,1,2,0:T(8,128)(2,1)} %collective-permute-done.1, bf16[8,8,128,128]{3,1,2,0:T(8,128)(2,1)S(1)} %copy-done, s32[22]{0:T(128)S(1)} %iota_add_fusion.3, s32[15,8]{1,0:T(8,128)S(1)} %copy.20, pred[15,8]{1,0:T(8,128)(4,1)S(1)} %copy.21), kind=kOutput, calls=%fused_computation.12 | convolution fusion | flops 94377120 | bytes 14746288 | tf_op jit(solution)/shard_map/bkxy,bka->aybx/dot_general | solution.py:45
  109.2 26.8 %copy.22 = bf16[15,22,128,128]{2,0,3,1:T(8,128)(2,1)} copy(bf16[15,22,128,128]{3,1,2,0:T(8,128)(2,1)} %fusion.7) | data formatting | bytes 21626880 | tf_op jit(solution)/shard_map/bkxy,bka->aybx/dot_general | solution.py:45
  136.1 8.0 %fusion = bf16[22,15,128,128]{3,1,2,0:T(8,128)(2,1)} fusion(bf16[7,8,128,128]{3,1,2,0:T(8,128)(2,1)} %collective-permute-done.1, bf16[8,8,128,128]{3,1,2,0:T(8,128)(2,1)S(1)} %copy-done, bf16[7,8,128,128]{3,1,2,0:T(8,128)(2,1)} %collective-permute-done, s32[15]{0:T(128)S(1)} %iota_add_fusion.4, s32[22,8]{1,0:T(8,128)S(1)} %copy.18), kind=kOutput, calls=%fused_computation.3 | convolution fusion | flops 103811664 | bytes 16581372 | tf_op jit(solution)/shard_map/akxy,akb->axby/dot_general | solution.py:38
  144.1 8.6 %bitcast_add_fusion = bf16[22,128,15,128]{3,2,1,0:T(8,128)(2,1)S(1)} fusion(bf16[15,22,128,128]{2,0,3,1:T(8,128)(2,1)} %copy.22, bf16[22,15,128,128]{3,1,2,0:T(8,128)(2,1)} %fusion), kind=kLoop, calls=%fused_computation | loop fusion | flops 5406720 | bytes 32440320 | tf_op jit(solution)/shard_map/add | solution.py:51
  152.6 3.6 %slice.60 = bf16[22,128,8,128]{3,2,1,0:T(8,128)(2,1)} slice(bf16[22,128,15,128]{3,2,1,0:T(8,128)(2,1)S(1)} %bitcast_add_fusion), slice={[0:22], [0:128], [0:8], [0:128]} | slice | bytes 11534336 | tf_op jit(solution)/shard_map/slice | solution.py:128
  156.2 6.9 %fusion.68 = (bf16[18,128,11,128]{3,2,1,0:T(8,128)(2,1)S(1)}, bf16[18,128,11,128]{3,2,1,0:T(8,128)(2,1)}) fusion(bf16[22,128,15,128]{3,2,1,0:T(8,128)(2,1)S(1)} %bitcast_add_fusion), kind=kLoop, calls=%fused_computation.88 | loop fusion | bytes 25952256 | tf_op jit(solution)/shard_map/slice | solution.py:101
  163.2 4.3 %dynamic-slice_bitcast_fusion = bf16[8,32,22,128]{1,0,3,2:T(8,128)(2,1)S(1)} fusion(bf16[22,128,8,128]{3,2,1,0:T(8,128)(2,1)} %slice.60, s32[]{:T(128)S(6)} %select_n.15), kind=kLoop, calls=%fused_computation.9 | loop fusion | bytes 2883588 | tf_op jit(solution)/shard_map/transpose | solution.py:129
  167.4 4.7 %fusion.69 = (bf16[4,32,18,128]{1,0,3,2:T(4,128)(2,1)}, bf16[4,32,18,128]{1,0,3,2:T(4,128)(2,1)}) fusion(bf16[8,32,22,128]{1,0,3,2:T(8,128)(2,1)S(1)} %dynamic-slice_bitcast_fusion), kind=kLoop, calls=%fused_computation.89 | loop fusion | bytes 2359296 | tf_op jit(solution)/shard_map/slice | solution.py:97
  172.2 6.0 %copy.66 = bf16[288,8,11,128]{3,1,2,0:T(8,128)(2,1)} copy(bf16[288,8,11,128]{3,2,1,0:T(8,128)(2,1)S(1)} %bitcast.86) | data formatting | bytes 12976128
  178.2 9.3 %copy.46 = bf16[2304,1408]{0,1:T(8,128)(2,1)} copy(bf16[2304,1408]{1,0:T(8,128)(2,1)} %bitcast.87) | data formatting | bytes 12976128 | tf_op jit(solution)/shard_map/reshape | solution.py:104
  187.4 9.7 %copy.65 = bf16[288,8,11,128]{3,1,2,0:T(8,128)(2,1)} copy(bf16[288,8,11,128]{3,2,1,0:T(8,128)(2,1)} %bitcast.85) | data formatting | bytes 12976128
  197.1 9.5 %copy.47 = bf16[2304,1408]{0,1:T(8,128)(2,1)} copy(bf16[2304,1408]{1,0:T(8,128)(2,1)} %bitcast.88) | data formatting | bytes 12976128 | tf_op jit(solution)/shard_map/reshape | solution.py:104
  206.6 6.5 %fusion.13 = f32[4,32,11,128]{3,1,2,0:T(8,128)S(1)} fusion(bf16[11,128,2304,1]{2,1,0,3:T(8,128)(2,1)} %bitcast.91, bf16[4,32,2304,1]{1,0,2,3:T(4,128)(2,1)S(1)} %bitcast.95), kind=kOutput, calls=%fused_computation.18 | convolution fusion | flops 830472192 | bytes 7798784 | tf_op jit(solution)/shard_map/dot_general | solution.py:105
  213.2 4.0 %fusion.11 = f32[4,32,11,128]{3,1,2,0:T(8,128)S(1)} fusion(bf16[11,128,2304,1]{2,1,0,3:T(8,128)(2,1)S(1)} %bitcast.90, bf16[4,32,2304,1]{1,0,2,3:T(4,128)(2,1)S(1)} %bitcast.94), kind=kOutput, calls=%fused_computation.16 | convolution fusion | flops 830472192 | bytes 7798784 | tf_op jit(solution)/shard_map/dot_general | solution.py:105
  219.8 45.6 %all-gather.5.cloned.1.call-done = bf16[8,8,128,128]{3,1,2,0:T(8,128)(2,1)} async-done(((bf16[8,8,32,128]{3,1,2,0:T(8,128)(2,1)}), bf16[8,8,128,128]{3,1,2,0:T(8,128)(2,1)}) %all-gather.5.cloned.1.call-update) | async-done | bytes 2097168 | tf_op jit(solution)/shard_map/all_gather | solution.py:132
  265.3 3.0 slice.65
  270.6 23.5 %collective-permute-done.2 = bf16[7,8,128,128]{3,1,2,0:T(8,128)(2,1)} collective-permute-done((bf16[7,8,128,128]{3,1,2,0:T(8,128)(2,1)}, bf16[7,8,128,128]{3,1,2,0:T(8,128)(2,1)}, u32[]{:S(2)}, u32[]{:S(2)}) %collective-permute-start.2) | collective-permute-done | bytes 1835040 | tf_op jit(solution)/shard_map/ppermute | solution.py:27
  294.1 4.5 %fusion.6 = bf16[15,8,32,128]{2,1,3,0:T(8,128)(2,1)} fusion(s32[]{:T(128)S(6)} %select_n.15, bf16[8,8,128,128]{3,1,2,0:T(8,128)(2,1)S(1)} %copy-done.1, bf16[7,8,128,128]{3,1,2,0:T(8,128)(2,1)} %collective-permute-done.2), kind=kLoop, calls=%fused_computation.11 | loop fusion | flops 1966080 | bytes 4915204 | tf_op jit(solution)/shard_map/transpose | solution.py:136
  298.6 4.7 %copy.29 = bf16[15,8,32,128]{3,1,2,0:T(8,128)(2,1)S(1)} copy(bf16[15,8,32,128]{2,1,3,0:T(8,128)(2,1)} %fusion.6) | data formatting | bytes 1966080 | tf_op jit(solution)/shard_map/transpose | solution.py:136
  306.8 5.2 %fusion.27 = f32[4,32,11,128]{3,1,2,0:T(8,128)S(1)} fusion(bf16[11,128,2304,1]{2,1,0,3:T(8,128)(2,1)} %bitcast.92, bf16[4,32,2304,1]{2,1,0,3:T(8,128)(2,1)} %reshape.82), kind=kOutput, calls=%fused_computation.36 | convolution fusion | flops 830472192 | bytes 7798784 | tf_op jit(solution)/shard_map/dot_general | solution.py:105
  313.2 5.0 %fusion.25 = f32[4,32,11,128]{3,1,2,0:T(8,128)S(1)} fusion(bf16[11,128,2304,1]{2,1,0,3:T(8,128)(2,1)} %bitcast.89, bf16[4,32,2304,1]{2,1,0,3:T(8,128)(2,1)S(1)} %reshape.83), kind=kOutput, calls=%fused_computation.34 | convolution fusion | flops 830472192 | bytes 7798784 | tf_op jit(solution)/shard_map/dot_general | solution.py:105
  (58 shorter events, 19.2 us)
Async XLA Ops:
  6.5 49.6 %all-gather.3.cloned.1.call-start = ((), (), s32[]{:S(2)}) async-start(), calls=%async_computation | async-start | bytes 2621440 | tf_op jit(solution)/shard_map/all_gather | solution.py:124
  8.6 56.5 %copy-start.7 = (s32[64,8]{0,1:T(8,128)S(1)}, s32[64,8]{0,1:T(8,128)}, u32[]{:S(2)}) copy-start(s32[64,8]{0,1:T(8,128)} %param.4) | copy-start | bytes 6148
  8.6 57.1 %copy-start.6 = (s32[64,8]{0,1:T(8,128)S(1)}, s32[64,8]{0,1:T(8,128)}, u32[]{:S(2)}) copy-start(s32[64,8]{0,1:T(8,128)} %param.5) | copy-start | bytes 6148
  8.6 256.7 %all-gather.5.cloned.1.call-start = ((), (), s32[]{:S(2)}) async-start(), calls=%async_computation.1 | async-start | bytes 2621440 | tf_op jit(solution)/shard_map/all_gather | solution.py:132
  56.1 45.8 %copy-start = (bf16[8,8,128,128]{3,1,2,0:T(8,128)(2,1)S(1)}, bf16[8,8,128,128]{3,1,2,0:T(8,128)(2,1)}, u32[]{:S(2)}) copy-start(bf16[8,8,128,128]{3,1,2,0:T(8,128)(2,1)} %all-gather.3.cloned.1.call-done) | copy-start | bytes 6291460
  60.4 41.4 %collective-permute-start.1 = (bf16[7,8,128,128]{3,1,2,0:T(8,128)(2,1)}, bf16[7,8,128,128]{3,1,2,0:T(8,128)(2,1)}, u32[]{:S(2)}, u32[]{:S(2)}) collective-permute-start(bf16[7,8,128,128]{3,1,2,0:T(8,128)(2,1)} %get-tuple-element.12), channel_id=1, source_target_pairs={{4,0},{8,4},{12,8},{16,12},{20,16},{24,20},{28,24},{5,1},{9,5},{13... | collective-permute-start | bytes 5505032 | tf_op jit(solution)/shard_map/ppermute | solution.py:19
  63.2 72.9 %collective-permute-start = (bf16[7,8,128,128]{3,1,2,0:T(8,128)(2,1)}, bf16[7,8,128,128]{3,1,2,0:T(8,128)(2,1)}, u32[]{:S(2)}, u32[]{:S(2)}) collective-permute-start(bf16[7,8,128,128]{3,1,2,0:T(8,128)(2,1)} %get-tuple-element.11), channel_id=1, source_target_pairs={{0,4},{4,8},{8,12},{12,16},{16,20},{20,24},{24,28},{1,5},{5,9},{9,... | collective-permute-start | bytes 5505032 | tf_op jit(solution)/shard_map/ppermute | solution.py:18
  197.1 9.5 %copy-start.5 = (bf16[4,32,18,128]{1,0,3,2:T(4,128)(2,1)S(1)}, bf16[4,32,18,128]{1,0,3,2:T(4,128)(2,1)}, u32[]{:S(2)}) copy-start(bf16[4,32,18,128]{1,0,3,2:T(4,128)(2,1)} %get-tuple-element.9) | copy-start | bytes 1769476
  206.6 6.5 %copy-start.2 = (bf16[2304,1408]{0,1:T(8,128)(2,1)S(1)}, bf16[2304,1408]{0,1:T(8,128)(2,1)}, u32[]{:S(2)}) copy-start(bf16[2304,1408]{0,1:T(8,128)(2,1)} %copy.47) | copy-start | bytes 19464196
  206.6 6.5 %copy-start.4 = (bf16[4,32,18,128]{1,0,3,2:T(4,128)(2,1)S(1)}, bf16[4,32,18,128]{1,0,3,2:T(4,128)(2,1)}, u32[]{:S(2)}) copy-start(bf16[4,32,18,128]{1,0,3,2:T(4,128)(2,1)} %get-tuple-element.10) | copy-start | bytes 1769476
  265.3 28.8 %copy-start.1 = (bf16[8,8,128,128]{3,1,2,0:T(8,128)(2,1)S(1)}, bf16[8,8,128,128]{3,1,2,0:T(8,128)(2,1)}, u32[]{:S(2)}) copy-start(bf16[8,8,128,128]{3,1,2,0:T(8,128)(2,1)} %all-gather.5.cloned.1.call-done) | copy-start | bytes 6291460
  268.3 25.7 %collective-permute-start.2 = (bf16[7,8,128,128]{3,1,2,0:T(8,128)(2,1)}, bf16[7,8,128,128]{3,1,2,0:T(8,128)(2,1)}, u32[]{:S(2)}, u32[]{:S(2)}) collective-permute-start(bf16[7,8,128,128]{3,1,2,0:T(8,128)(2,1)} %slice.65), channel_id=1, source_target_pairs={{0,4},{4,8},{8,12},{12,16},{16,20},{20,24},{24,28},{1,5},{5,9},{9,... | collective-permute-start | bytes 5505032 | tf_op jit(solution)/shard_map/ppermute | solution.py:27
  298.6 5.9 %copy-start.3 = (bf16[8,8,32,128]{3,1,2,0:T(8,128)(2,1)S(1)}, bf16[8,8,32,128]{3,1,2,0:T(8,128)(2,1)}, u32[]{:S(2)}) copy-start(bf16[8,8,32,128]{3,1,2,0:T(8,128)(2,1)} %fusion.24) | copy-start | bytes 1572868
Sparse Core Ops, SparseCore 0:
  8.9 47.1 all-gather.2
  219.9 45.4 all-gather.4
where the time goes:
time: 328 us; the launch traced here: 327 us
  waiting for transfers between devices  152 us (46%)
  local copies, waits for them, and re-layouts  99.6 us (30%)
  matrix products  40.7 us (12%)
  other arithmetic  14.2 us (4%)
  between operations  13.6 us (4%)
  starting transfers between devices  6.63 us (2%)
    all_gather x1, waiting for transfers between devices, per_device(): whole_blocks = lax.all_gather(upper_blocks, 'col', axis=2, tiled=True)  47.4 us
    all_gather x1, waiting for transfers between devices, per_device(): whole_square = lax.all_gather(square_half, 'col', axis=2, tiled=True)  45.6 us
    ppermute x1, waiting for transfers between devices, padded(): after = lax.ppermute(leading, axis, down)  35.9 us
    dot_general x1, local copies, waits for them, and re-layouts, band_right(): jnp.einsum('bkxy,bka->aybx', blocks[rim_rows:], lower_hit.astype(jnp.bflo...  26.8 us
    ppermute x1, waiting for transfers between devices, from_behind(): lax.ppermute(value, axis, [(source, source + steps) for source in range(l...  23.5 us
    dot_general x4, matrix products, group_products(): product = jnp.dot(left_part, right_part, preferred_element_type=jnp.float32)  20.7 us
    reshape x2, local copies, waits for them, and re-layouts, group_products(): right_part = right_part.reshape(span_rows * B, width_cols * B)  18.8 us
    unnamed x19, local copies, waits for them, and re-layouts  17.8 us
  transfers between devices with their start and end apart: 5, of which 4 were waited for; matrix products, arithmetic and copies ran while one was open for 11% of the time, Pallas kernels for 0%

commit v1 on v0

--- a/solution.py
+++ b/solution.py
@@ -129,7 +129,27 @@
     left_rows = jnp.transpose(own_band, (2, 3, 0, 1))
     square = group_products(left_rows, right_band, own_filter, row_first)
     square_half = square.astype(jnp.bfloat16)
-    whole_square = lax.all_gather(square_half, "col", axis=2, tiled=True)
+    count_2, mine, width_2 = (lax.axis_size("col"), lax.axis_index("col"), square_half.shape[2])
+    forward = [(i_2, (i_2 + 1) % count_2) for i_2 in range(count_2)]
+    backward = [(i_2, (i_2 - 1) % count_2) for i_2 in range(count_2)]
+    whole_square = jnp.zeros(
+        (*square_half.shape[:2], count_2 * width_2, *square_half.shape[2 + 1 :]), square_half.dtype
+    )
+    whole_square = lax.dynamic_update_slice_in_dim(
+        whole_square, square_half, mine * width_2, axis=2
+    )
+    from_left = from_right = square_half
+    halfway = count_2 // 2
+    for step in range(1, halfway + 1):
+        from_left = lax.ppermute(from_left, "col", forward)
+        whole_square = lax.dynamic_update_slice_in_dim(
+            whole_square, from_left, (mine - step) % count_2 * width_2, axis=2
+        )
+        if step < count_2 - halfway:
+            from_right = lax.ppermute(from_right, "col", backward)
+            whole_square = lax.dynamic_update_slice_in_dim(
+                whole_square, from_right, (mine + step) % count_2 * width_2, axis=2
+            )
     earlier = from_behind(whole_square[row_count - rim_rows :], "row", 1)
     joined = jnp.concatenate([earlier, whole_square], axis=0)
     mirror_cols = lax.dynamic_slice_in_dim(joined, col_first, quarter, 3)

time: 328 us -> 858 us (2.62)
  local copies, waits for them, and re-layouts: 99.6 us -> 649 us
  waiting for transfers between devices: 152 us -> 123 us
    dynamic_update_slice x0 -> x4, local copies, waits for them, and re-layouts: none -> 541 us  [the longest x2 339 us: per_device(): lax.dynamic_update_slice_in_dim(whole_square, from_left, (mine - step) %...]
    all_gather x1 -> x0, waiting for transfers between devices: 45.6 us -> none  [per_device(): whole_square = lax.all_gather(square_half, 'col', axis=2, tiled=True)]
    ppermute x0 -> x3, local copies, waits for them, and re-layouts: none -> 10.2 us  [the longest x2 6.83 us: per_device(): from_left = lax.ppermute(from_left, 'col', forward)]
    unnamed x19 -> x15, local copies, waits for them, and re-layouts: 17.8 us -> 17.7 us
  transfers between devices with their start and end apart: 5 -> 7, of which waited for: 4 -> 4; matrix products, arithmetic and copies ran while one was open for 11% -> 49% of each run, Pallas kernels for 0% -> 0%
where the time goes in v1:
time: 858 us; the launch traced here: 849 us
  local copies, waits for them, and re-layouts  649 us (76%)
  waiting for transfers between devices  123 us (14%)
  matrix products  43.2 us (5%)
  between operations  13.9 us (2%)
  starting transfers between devices  10.6 us (1%)
  other arithmetic  9.72 us (1%)
    dynamic_update_slice x2, local copies, waits for them, and re-layouts, per_device(): lax.dynamic_update_slice_in_dim(whole_square, from_left, (mine - step) %...  339 us
    dynamic_update_slice x1, local copies, waits for them, and re-layouts, per_device(): lax.dynamic_update_slice_in_dim(whole_square, from_right, (mine + step) %...  170 us
    all_gather x1, waiting for transfers between devices, per_device(): whole_blocks = lax.all_gather(upper_blocks, 'col', axis=2, tiled=True)  47.5 us
    ppermute x1, waiting for transfers between devices, padded(): after = lax.ppermute(leading, axis, down)  35.9 us
    dynamic_update_slice x1, local copies, waits for them, and re-layouts, per_device(): lax.dynamic_update_slice_in_dim(whole_square, square_half, mine * width_2...  32.1 us
    ppermute x1, waiting for transfers between devices, from_behind(): lax.ppermute(value, axis, [(source, source + steps) for source in range(l...  31.6 us
    dot_general x1, local copies, waits for them, and re-layouts, band_right(): jnp.einsum('bkxy,bka->aybx', blocks[rim_rows:], lower_hit.astype(jnp.bflo...  26.9 us
    dot_general x4, matrix products, group_products(): product = jnp.dot(left_part, right_part, preferred_element_type=jnp.float32)  21 us
  transfers between devices with their start and end apart: 7, of which 4 were waited for; matrix products, arithmetic and copies ran while one was open for 49% of the time, Pallas kernels for 0%

profile of v1, /device:TPU:4, one launch (start us, length us, event | category | flops | bytes accessed | tf_op | source)
XLA Modules:
  0.0 848.7 jit_solution(4105797034062088537)
XLA Ops:
  8.6 47.5 %all-gather.2.cloned.1.call-done = bf16[8,8,128,128]{3,1,2,0:T(8,128)(2,1)} async-done(((bf16[8,8,32,128]{3,1,2,0:T(8,128)(2,1)}), bf16[8,8,128,128]{3,1,2,0:T(8,128)(2,1)}) %all-gather.2.cloned.1.call-update) | async-done | bytes 2097168 | tf_op jit(solution)/shard_map/all_gather | solution.py:124
  56.1 4.3 fusion.74
  66.0 35.9 %collective-permute-done.1 = bf16[7,8,128,128]{3,1,2,0:T(8,128)(2,1)} collective-permute-done((bf16[7,8,128,128]{3,1,2,0:T(8,128)(2,1)}, bf16[7,8,128,128]{3,1,2,0:T(8,128)(2,1)}, u32[]{:S(2)}, u32[]{:S(2)}) %collective-permute-start.1) | collective-permute-done | bytes 1835040 | tf_op jit(solution)/shard_map/ppermute | solution.py:19
  101.9 7.3 fusion.6
  109.2 26.9 %copy.25 = bf16[15,22,128,128]{2,0,3,1:T(8,128)(2,1)} copy(bf16[15,22,128,128]{3,1,2,0:T(8,128)(2,1)} %fusion.6) | data formatting | bytes 21626880 | tf_op jit(solution)/shard_map/bkxy,bka->aybx/dot_general | solution.py:45
  136.1 8.1 fusion
  144.1 8.6 %bitcast_add_fusion = bf16[22,128,15,128]{3,2,1,0:T(8,128)(2,1)S(1)} fusion(bf16[15,22,128,128]{2,0,3,1:T(8,128)(2,1)} %copy.25, bf16[22,15,128,128]{3,1,2,0:T(8,128)(2,1)} %fusion), kind=kLoop, calls=%fused_computation | loop fusion | flops 5406720 | bytes 32440320 | tf_op jit(solution)/shard_map/add | solution.py:51
  156.3 7.1 fusion.72
  163.5 4.3 dynamic-slice_bitcast_fusion
  167.7 4.7 fusion.73
  172.4 6.0 copy.72
  178.4 9.3 %copy.52 = bf16[2304,1408]{0,1:T(8,128)(2,1)} copy(bf16[2304,1408]{1,0:T(8,128)(2,1)} %bitcast.87) | data formatting | bytes 12976128 | tf_op jit(solution)/shard_map/reshape | solution.py:104
  187.7 9.7 %copy.71 = bf16[288,8,11,128]{3,1,2,0:T(8,128)(2,1)} copy(bf16[288,8,11,128]{3,2,1,0:T(8,128)(2,1)} %bitcast.85) | data formatting | bytes 12976128
  197.4 9.4 %copy.53 = bf16[2304,1408]{0,1:T(8,128)(2,1)} copy(bf16[2304,1408]{1,0:T(8,128)(2,1)} %bitcast.88) | data formatting | bytes 12976128 | tf_op jit(solution)/shard_map/reshape | solution.py:104
  206.8 6.9 fusion.12
  213.7 4.0 fusion.10
  224.1 7.6 collective-permute-done.2
  235.6 32.1 %dynamic_update_slice.12 = bf16[8,8,128,128]{2,1,3,0:T(8,128)(2,1)S(1)} dynamic-update-slice(bf16[8,8,128,128]{2,1,3,0:T(8,128)(2,1)S(1)} %broadcast_in_dim.2, bf16[8,8,32,128]{2,1,3,0:T(8,128)(2,1)} %copy.32, s32[]{:T(128)} %constant.46.clone.1, s32[]{:T(128)} %constant.46.clone.1, s32[]{:T(128)S(6)} %select_n.40, s32[]{:T(128)} %constant.46.clone.1) | dynamic-update-slice | bytes 1048580 | tf_op jit(solution)/shard_map/dynamic_update_slice | solution.py:138
  271.1 169.7 %dynamic_update_slice.13 = bf16[8,8,128,128]{2,1,3,0:T(8,128)(2,1)S(1)} dynamic-update-slice(bf16[8,8,128,128]{2,1,3,0:T(8,128)(2,1)S(1)} %dynamic_update_slice.12, bf16[8,8,32,128]{2,1,3,0:T(8,128)(2,1)} %copy.33, s32[]{:T(128)} %constant.46.clone.1, s32[]{:T(128)} %constant.46.clone.1, s32[]{:T(128)S(6)} %select_n.43, s32[]{:T(128)} %constant.46.clone.1) | dynamic-update-slice | bytes 1048580 | tf_op jit(solution)/shard_map/dynamic_update_slice | solution.py:145
  444.2 169.7 %dynamic_update_slice.14 = bf16[8,8,128,128]{2,1,3,0:T(8,128)(2,1)S(1)} dynamic-update-slice(bf16[8,8,128,128]{2,1,3,0:T(8,128)(2,1)S(1)} %dynamic_update_slice.13, bf16[8,8,32,128]{2,1,3,0:T(8,128)(2,1)} %copy.34, s32[]{:T(128)} %constant.46.clone.1, s32[]{:T(128)} %constant.46.clone.1, s32[]{:T(128)S(6)} %select_n.45, s32[]{:T(128)} %constant.46.clone.1) | dynamic-update-slice | bytes 1048580 | tf_op jit(solution)/shard_map/dynamic_update_slice | solution.py:150
  617.4 169.7 %dynamic_update_slice.15 = bf16[8,8,128,128]{2,1,3,0:T(8,128)(2,1)S(1)} dynamic-update-slice(bf16[8,8,128,128]{2,1,3,0:T(8,128)(2,1)S(1)} %dynamic_update_slice.14, bf16[8,8,32,128]{2,1,3,0:T(8,128)(2,1)} %copy.35, s32[]{:T(128)} %constant.46.clone.1, s32[]{:T(128)} %constant.46.clone.1, s32[]{:T(128)S(6)} %select_n.47, s32[]{:T(128)} %constant.46.clone.1) | dynamic-update-slice | bytes 1048580 | tf_op jit(solution)/shard_map/dynamic_update_slice | solution.py:145
  790.9 31.6 %collective-permute-done.5 = bf16[7,8,128,128]{2,1,3,0:T(8,128)(2,1)} collective-permute-done((bf16[7,8,128,128]{2,1,3,0:T(8,128)(2,1)}, bf16[7,8,128,128]{2,1,3,0:T(8,128)(2,1)}, u32[]{:S(2)}, u32[]{:S(2)}) %collective-permute-start.5) | collective-permute-done | bytes 1835040 | tf_op jit(solution)/shard_map/ppermute | solution.py:27
  828.1 5.2 fusion.30
  834.5 5.0 fusion.28
  (64 shorter events, 44.3 us)
Async XLA Ops:
  6.5 49.6 %all-gather.2.cloned.1.call-start = ((), (), s32[]{:S(2)}) async-start(), calls=%async_computation | async-start | bytes 2621440 | tf_op jit(solution)/shard_map/all_gather | solution.py:124
  8.6 56.5 %copy-start.5 = (s32[64,8]{0,1:T(8,128)S(1)}, s32[64,8]{0,1:T(8,128)}, u32[]{:S(2)}) copy-start(s32[64,8]{0,1:T(8,128)} %param.4) | copy-start | bytes 6148
  8.6 57.0 %copy-start.4 = (s32[64,8]{0,1:T(8,128)S(1)}, s32[64,8]{0,1:T(8,128)}, u32[]{:S(2)}) copy-start(s32[64,8]{0,1:T(8,128)} %param.5) | copy-start | bytes 6148
  56.1 45.8 %copy-start = (bf16[8,8,128,128]{3,1,2,0:T(8,128)(2,1)S(1)}, bf16[8,8,128,128]{3,1,2,0:T(8,128)(2,1)}, u32[]{:S(2)}) copy-start(bf16[8,8,128,128]{3,1,2,0:T(8,128)(2,1)} %all-gather.2.cloned.1.call-done) | copy-start | bytes 6291460
  60.4 41.4 %collective-permute-start.1 = (bf16[7,8,128,128]{3,1,2,0:T(8,128)(2,1)}, bf16[7,8,128,128]{3,1,2,0:T(8,128)(2,1)}, u32[]{:S(2)}, u32[]{:S(2)}) collective-permute-start(bf16[7,8,128,128]{3,1,2,0:T(8,128)(2,1)} %get-tuple-element.12), channel_id=1, source_target_pairs={{4,0},{8,4},{12,8},{16,12},{20,16},{24,20},{28,24},{5,1},{9,5},{13... | collective-permute-start | bytes 5505032 | tf_op jit(solution)/shard_map/ppermute | solution.py:19
  63.2 72.9 %collective-permute-start = (bf16[7,8,128,128]{3,1,2,0:T(8,128)(2,1)}, bf16[7,8,128,128]{3,1,2,0:T(8,128)(2,1)}, u32[]{:S(2)}, u32[]{:S(2)}) collective-permute-start(bf16[7,8,128,128]{3,1,2,0:T(8,128)(2,1)} %get-tuple-element.11), channel_id=1, source_target_pairs={{0,4},{4,8},{8,12},{12,16},{16,20},{20,24},{24,28},{1,5},{5,9},{9,... | collective-permute-start | bytes 5505032 | tf_op jit(solution)/shard_map/ppermute | solution.py:18
  197.4 9.4 %copy-start.3 = (bf16[4,32,18,128]{1,0,3,2:T(4,128)(2,1)S(1)}, bf16[4,32,18,128]{1,0,3,2:T(4,128)(2,1)}, u32[]{:S(2)}) copy-start(bf16[4,32,18,128]{1,0,3,2:T(4,128)(2,1)} %get-tuple-element.9) | copy-start | bytes 1769476
  206.8 6.9 copy-start.1
  206.8 6.9 copy-start.2
  220.3 11.5 %collective-permute-start.2 = (bf16[8,8,32,128]{3,1,2,0:T(8,128)(2,1)}, bf16[8,8,32,128]{3,1,2,0:T(8,128)(2,1)}, u32[]{:S(2)}, u32[]{:S(2)}) collective-permute-start(bf16[8,8,32,128]{3,1,2,0:T(8,128)(2,1)} %fusion.27), channel_id=1, source_target_pairs={{0,1},{1,2},{2,3},{3,0},{4,5},{5,6},{6,7},{7,4},{8,9},{9,10},{10,1... | collective-permute-start | bytes 1572872 | tf_op jit(solution)/shard_map/ppermute | solution.py:144
  220.3 220.5 %collective-permute-start.3 = (bf16[8,8,32,128]{3,1,2,0:T(8,128)(2,1)}, bf16[8,8,32,128]{3,1,2,0:T(8,128)(2,1)}, u32[]{:S(2)}, u32[]{:S(2)}) collective-permute-start(bf16[8,8,32,128]{3,1,2,0:T(8,128)(2,1)} %fusion.27), channel_id=1, source_target_pairs={{0,3},{1,0},{2,1},{3,2},{4,7},{5,4},{6,5},{7,6},{8,11},{9,8},{10,9... | collective-permute-start | bytes 1572872 | tf_op jit(solution)/shard_map/ppermute | solution.py:149
  231.7 382.2 %collective-permute-start.4 = (bf16[8,8,32,128]{3,1,2,0:T(8,128)(2,1)}, bf16[8,8,32,128]{3,1,2,0:T(8,128)(2,1)}, u32[]{:S(2)}, u32[]{:S(2)}) collective-permute-start(bf16[8,8,32,128]{3,1,2,0:T(8,128)(2,1)} %collective-permute-done.2), channel_id=1, source_target_pairs={{0,1},{1,2},{2,3},{3,0},{4,5},{5,6},{6,7},{7,4},{8,9},{9,10},{10,1... | collective-permute-start | bytes 1572872 | tf_op jit(solution)/shard_map/ppermute | solution.py:144
  788.5 34.1 %collective-permute-start.5 = (bf16[7,8,128,128]{2,1,3,0:T(8,128)(2,1)}, bf16[7,8,128,128]{2,1,3,0:T(8,128)(2,1)}, u32[]{:S(2)}, u32[]{:S(2)}) collective-permute-start(bf16[7,8,128,128]{2,1,3,0:T(8,128)(2,1)} %slice.65), channel_id=1, source_target_pairs={{0,4},{4,8},{8,12},{12,16},{16,20},{20,24},{24,28},{1,5},{5,9},{9,... | collective-permute-start | bytes 5505032 | tf_op jit(solution)/shard_map/ppermute | solution.py:27
Sparse Core Ops, SparseCore 0:
  8.9 47.1 all-gather.1
